TPU v7x, 256 devices: a whole 4x4x8 slice. The times are simulated.
256 devices in a mesh: fsdp: 32 (over z, x_hi, core), tensor: 8 (over x_lo, y).
Axes of the slice: x: 4 (x_hi: 2, x_lo: 2; x = x_hi * 2 + x_lo), y: 4, z: 8, core: 2. Of those that a mesh axis runs over, the one named last changes fastest.
Arguments:
- tokens: bfloat16 [49152, 8192], P(('fsdp', 'tensor'))
- gain: bfloat16 [8192], replicated, may hold values from 0.5 to 1.5
- kv_weight: bfloat16 [8192, 2048], P('fsdp', 'tensor'), may hold values from -0.09375 to 0.09375
- block_mask: int32 [64, 16], P('fsdp', 'tensor'), may hold values from 0 to 1
- cotangent: bfloat16 [49152, 2048], P('fsdp', 'tensor'), may hold values from -0.02734375 to 0.02734375
Outputs:
- projected: bfloat16 [49152, 2048], P('fsdp', 'tensor')
- weight_grad: float32 [8192, 2048], P('fsdp', 'tensor')
All inputs are finite; a program needn't handle non-finite values.
Results may differ from a plain program's by a relative error of at most 0.005.
Values may be sent and summed in bfloat16 or wider, within the bound.
A program may use at most 128 MiB of HBM per device.

v0:
```python
import jax
import jax.numpy as jnp
from jax import lax
from jax.sharding import PartitionSpec as P


def normalize(rows, gain):
    values = rows.astype(jnp.float32)
    square = jnp.mean(values * values, axis=-1, keepdims=True)
    return (values * lax.rsqrt(square + 1e-05) * gain.astype(jnp.float32)).astype(jnp.bfloat16)


def apply_mask(panel, mask):
    rows, cols = panel.shape
    mrows, mcols = mask.shape
    shaped = panel.reshape(mrows, rows // mrows, mcols, cols // mcols)
    kept = shaped * mask[:, None, :, None].astype(panel.dtype)
    return kept.reshape(rows, cols)


def per_device(tokens, gain, kv_weight, block_mask, cotangent):
    group = lax.all_gather(normalize(tokens, gain), "tensor", axis=0, tiled=True)
    columns = group
    total = jnp.dot(
        columns,
        apply_mask(
            lax.all_gather(kv_weight, "fsdp", axis=0, tiled=True),
            lax.all_gather(block_mask, "fsdp", axis=0, tiled=True),
        ),
        preferred_element_type=jnp.float32,
    )
    projected = total.astype(jnp.bfloat16)
    columns = group
    summed = lax.psum_scatter(
        lax.dot_general(
            columns, cotangent, (((0,), (0,)), ((), ())), preferred_element_type=jnp.float32
        ),
        "fsdp",
        scatter_dimension=0,
        tiled=True,
    )
    weight_grad = apply_mask(summed, block_mask)
    return (projected, weight_grad)


def solution(mesh):
    return jax.shard_map(
        per_device,
        mesh=mesh,
        in_specs=(
            P(("fsdp", "tensor"), None),
            P(),
            P("fsdp", "tensor"),
            P("fsdp", "tensor"),
            P("fsdp", "tensor"),
        ),
        out_specs=(P("fsdp", "tensor"), P("fsdp", "tensor")),
        check_vma=False,
    )
```

profile of v0, /device:TPU:1, one launch (start us, length us, event | category | flops | bytes accessed | tf_op | source)
XLA Modules:
  0.0 517.7 jit_solution(9037868814021527761)
XLA Ops:
  7.2 0.0 copy-start
  7.2 0.0 all-gather.4.cloned.1.call-start
  7.2 0.8 convert_element_type.21
  8.0 2.6 fusion
  10.6 4.5 fusion.2
  15.1 0.0 all-gather.4.cloned.1.call-update
  15.1 0.0 all-gather.6.cloned.1.call-start
  15.2 0.7 all-gather.6.cloned.1.call-update
  15.9 0.0 reduce-scatter.2.cloned.1.call-start
  15.9 254.9 %all-gather.4.cloned.1.call-done = bf16[1536,8192]{1,0:T(8,128)(2,1)} async-done(((bf16[192,8192]{1,0:T(8,128)(2,1)}), bf16[1536,8192]{1,0:T(8,128)(2,1)}) %all-gather.4.cloned.1.call-update) | async-done | bytes 25165840 | tf_op jit(solution)/shard_map/all_gather | solution.py:22
  270.8 0.0 copy-done
  270.8 13.9 %fusion.6 = f32[8192,256]{1,0:T(8,128)} fusion(bf16[1536,8192]{1,0:T(8,128)(2,1)} %all-gather.4.cloned.1.call-done, bf16[1536,256]{1,0:T(8,128)(2,1)S(1)} %copy-done), kind=kOutput, calls=%fused_computation.11 | convolution fusion | flops 6442450944 | bytes 34340864 | tf_op jit(solution)/shard_map/dot_general | solution.py:35
  284.8 0.0 copy-start.1
  284.8 0.0 reduce-scatter.2.cloned.1.call-update
  284.8 0.7 copy-done.1
  285.4 42.3 %all-gather = s32[32,2,2]{2,1,0:T(2,128)S(1)} all-gather(s32[1,2,2]{2,1,0:T(2,128)S(1)} %bitcast.19), channel_id=1, replica_groups=mesh['fsdp'=32,'tensor'=8] {'fsdp'}, dimensions={0}, use_global_device_ids=true | all-gather | bytes 528 | tf_op jit(solution)/shard_map/all_gather | solution.py:28
  327.7 0.1 copy.13
  327.8 0.1 copy.16
  328.0 31.8 %all-gather.6.cloned.1.call-done = bf16[8192,256]{1,0:T(8,128)(2,1)} async-done(((bf16[256,256]{1,0:T(8,128)(2,1)}), bf16[8192,256]{1,0:T(8,128)(2,1)}) %all-gather.6.cloned.1.call-update) | async-done | bytes 4194320 | tf_op jit(solution)/shard_map/all_gather | solution.py:27
  359.7 2.2 mul.46
  362.0 13.5 %fusion.5 = bf16[1536,256]{1,0:T(8,128)(2,1)} fusion(bf16[1536,8192]{1,0:T(8,128)(2,1)} %all-gather.4.cloned.1.call-done, bf16[8192,256]{1,0:T(8,128)(2,1)} %all-gather.6.cloned.1.call-done, bf16[1024,8,2,128]{3,2,1,0:T(2,128)(2,1)S(1)} %bitcast.16), kind=kOutput, calls=%fused_computation.8 | convolution fusion | flops 6444941312 | bytes 34340864 | tf_op jit(solution)/shard_map/dot_general | solution.py:24
  375.5 133.8 %reduce-scatter.2.cloned.1.call-done = f32[256,256]{1,0:T(8,128)} async-done(((f32[8192,256]{1,0:T(8,128)}), f32[256,256]{1,0:T(8,128)}) %reduce-scatter.2.cloned.1.call-update) | async-done | bytes 262160 | tf_op jit(solution)/shard_map/reduce_scatter | solution.py:34
  509.3 0.1 mul.49
  509.5 1.7 bitcast_multiply_fusion.4
  (3 shorter events, 0.0 us)
Async XLA Ops:
  7.2 263.7 %copy-start = (bf16[1536,256]{1,0:T(8,128)(2,1)S(1)}, bf16[1536,256]{1,0:T(8,128)(2,1)}, u32[]{:S(2)}) copy-start(bf16[1536,256]{1,0:T(8,128)(2,1)} %param.9) | copy-start | bytes 2359300
  7.2 263.6 %all-gather.4.cloned.1.call-start = ((), (), s32[]{:S(2)}) async-start(), calls=%async_computation.1 | async-start | bytes 28311552 | tf_op jit(solution)/shard_map/all_gather | solution.py:22
  15.1 344.6 %all-gather.6.cloned.1.call-start = ((), (), s32[]{:S(2)}) async-start(), calls=%async_computation.2 | async-start | bytes 4325376 | tf_op jit(solution)/shard_map/all_gather | solution.py:27
  15.9 493.4 %reduce-scatter.2.cloned.1.call-start = ((), (), s32[]{:S(2)}) async-start(), calls=%async_computation.3 | async-start | bytes 8650752 | tf_op jit(solution)/shard_map/reduce_scatter | solution.py:34
  284.8 0.7 copy-start.1
Sparse Core Ops, SparseCore 0:
  15.2 255.5 all-gather.3
  273.6 86.0 all-gather.5
  364.1 145.1 reduce-scatter.1
where the time goes:
time: 521 us; the launch traced here: 518 us
  waiting for transfers between devices  421 us (81%)
  blocking collectives  42.3 us (8%)
  matrix products  27.5 us (5%)
  between operations  13.8 us (3%)
  other arithmetic  9.57 us (2%)
    all_gather x1, waiting for transfers between devices, per_device(): lax.all_gather(normalize(tokens, gain), 'tensor', axis=0, tiled=True)  255 us
    reduce_scatter x1, waiting for transfers between devices, per_device(): lax.psum_scatter(lax.dot_general(columns, cotangent, (((0,), (0,)), ((),...  134 us
    all_gather x1, blocking collectives, per_device(): lax.all_gather(block_mask, 'fsdp', axis=0, tiled=True)  42.3 us
    all_gather x1, waiting for transfers between devices, per_device(): lax.all_gather(kv_weight, 'fsdp', axis=0, tiled=True)  31.8 us
    dot_general x1, matrix products, per_device(): lax.dot_general(columns, cotangent, (((0,), (0,)), ((), ())), preferred_e...  13.9 us
    dot_general x1, matrix products, per_device(): jnp.dot(columns, apply_mask(lax.all_gather(kv_weight, 'fsdp', axis=0, til...  13.5 us
  transfers between devices with their start and end apart: 3, of which 3 were waited for; matrix products, arithmetic and copies ran while one was open for 6% of the time, Pallas kernels for 0%

commit v1 on v0

v1 whole, which is shorter than its diff:
```python
import jax
import jax.numpy as jnp
from jax import lax
from jax.experimental import pallas as pl
from jax.experimental.pallas import tpu as pltpu
from jax.sharding import PartitionSpec as P

MESH = pl.DeviceIdType.MESH
NZ, NX, NC, NY = 8, 4, 2, 4
BLOCK = 128


def kernel(
    tokens, gain, weight, mask, cot, proj, grad,
    normed, scale, masked, cot_in, cot_t, part, core_in, keep, x_out, x_in,
    z_out, z_in, acc, p_out, p_in,
    y_send, y_recv, w_send, w_recv, wz_send, wz_recv, wd_send, wd_recv,
    c_send, c_recv, x_send, x_recv, z_send, z_recv, o_send, o_recv,
):
    rows = tokens.shape[0]
    group = NY * rows
    side = weight.shape[0]
    wide = 4 * side
    f, t = lax.axis_index("fsdp"), lax.axis_index("tensor")
    z, xh, c = lax.div(f, 4), lax.rem(lax.div(f, 2), 2), lax.rem(f, 2)
    xl, y = lax.div(t, NY), lax.rem(t, NY)
    x = xh * 2 + xl
    q = x * 2 + c
    yp, ym, y2 = lax.rem(y + 1, NY), lax.rem(y + 3, NY), lax.rem(y + 2, NY)
    zp, zm = lax.rem(z + 1, NZ), lax.rem(z + NZ - 1, NZ)

    def dev(zz, xx, cc, yy):
        return ((zz * 2 + lax.div(xx, 2)) * 2 + cc, lax.rem(xx, 2) * NY + yy)

    def chunk(k):
        return lax.rem(z + 1 + k, NZ)

    def copy(src, dst, send, recv, to):
        return pltpu.make_async_remote_copy(
            src_ref=src, dst_ref=dst, send_sem=send, recv_sem=recv, device_id=to, device_id_type=MESH
        )

    sibling = dev(z, x, 1 - c, y)
    beside = dev(z, xh * 2 + 1 - xl, c, y)
    up, down = dev(z, x, c, yp), dev(z, x, c, ym)

    barrier = pltpu.get_barrier_semaphore()

    def greet(to):
        pl.semaphore_signal(barrier, inc=1, device_id=to, device_id_type=MESH)

    greet(up)
    greet(down)
    for r in range(1, 8):
        p = lax.rem(q + r, 8)
        greet(dev(z, lax.div(p, 2), lax.rem(p, 2), y))
        greet(dev(lax.rem(z + r, NZ), x, c, y))

    own_j = xh * 2 + c
    for a in range(side // BLOCK):
        for b in range(side // BLOCK):
            at = (pl.ds(a * BLOCK, BLOCK), pl.ds(b * BLOCK, BLOCK))
            m = mask[a, b].astype(jnp.float32)
            masked[z, own_j, xl, at[0], at[1]] = (weight[at].astype(jnp.float32) * m).astype(jnp.bfloat16)

    @pl.loop(0, rows // 16)
    def _(r):
        at = pl.ds(pl.multiple_of(r * 16, 16), 16)
        v = tokens[at, :].astype(jnp.float32)
        square = jnp.mean(v * v, axis=-1, keepdims=True)
        scale[at, :] = jnp.broadcast_to(lax.rsqrt(square + 1e-05), (16, side))

    def normalize(k):
        zc = chunk(k)

        @pl.loop(0, 4)
        def _(j):
            at = pl.ds(pl.multiple_of(zc * wide + j * side, side), side)
            v = tokens[:, at].astype(jnp.float32)
            g = gain[:, at].astype(jnp.float32)
            normed[zc, y, j] = (v * scale[...] * g).astype(jnp.bfloat16)

    def direct(k, way):
        zc = chunk(k)
        return copy(
            normed.at[zc, y], normed.at[zc, y], y_send.at[k, way], y_recv.at[k, way], down if way else up
        )

    def direct_in(k, way):
        zc = chunk(k)
        slot = normed.at[zc, yp if way else ym]
        return copy(slot, slot, y_send.at[k, way], y_recv.at[k, way], up)

    def forward(k, way):
        zc = chunk(k)
        slot = normed.at[zc, yp if way else ym, pl.ds(2 * way, 2)]
        return copy(slot, slot, y_send.at[k, 2 + way], y_recv.at[k, 2 + way], down if way else up)

    def forward_in(k, way):
        zc = chunk(k)
        slot = normed.at[zc, y2, pl.ds(2 * way, 2)]
        return copy(slot, slot, y_send.at[k, 2 + way], y_recv.at[k, 2 + way], up)

    def w_first(r):
        p = lax.rem(q + r, 8)
        slot = masked.at[z, own_j, xl]
        return copy(slot, slot, w_send.at[r], w_recv.at[r], dev(z, lax.div(p, 2), lax.rem(p, 2), y))

    def w_first_in(r):
        p = lax.rem(q + 8 - r, 8)
        px, pc = lax.div(p, 2), lax.rem(p, 2)
        slot = masked.at[z, lax.div(px, 2) * 2 + pc, lax.rem(px, 2)]
        return copy(slot, slot, w_send.at[r], w_recv.at[r], sibling)

    def w_ring(offset, to, at_receiver):
        slot = masked.at[lax.rem(z + offset, NZ), pl.ds(2 * c, 2)]
        return copy(slot, slot, wz_send.at[at_receiver], wz_recv.at[at_receiver], dev(to, x, c, y))

    def w_ring_in(offset):
        return w_ring(offset, zp, offset)

    def w_share(offset):
        slot = masked.at[lax.rem(z + offset, NZ), pl.ds(2 * c, 2)]
        return copy(slot, slot, wd_send.at[offset], wd_recv.at[offset], sibling)

    def w_share_in(offset):
        slot = masked.at[lax.rem(z + offset, NZ), pl.ds(2 * (1 - c), 2)]
        return copy(slot, slot, wd_send.at[offset], wd_recv.at[offset], sibling)

    def cot_swap():
        src = cot.at[pl.ds(pl.multiple_of((1 - xl) * group, group), group)]
        return copy(src, cot_in, o_send.at[0], o_recv.at[0], beside)

    def proj_swap():
        return copy(p_out, p_in, o_send.at[1], o_recv.at[1], beside)

    def core_swap(k):
        return copy(
            part.at[lax.rem(k, 2), pl.ds(0, 2)], core_in.at[k], c_send.at[k], c_recv.at[k], sibling
        )

    def x_term(k, d):
        xd = lax.rem(x + d, NX)
        return copy(
            x_out.at[k, d - 1], x_in.at[k, d - 1], x_send.at[k, d - 1], x_recv.at[k, d - 1], dev(z, xd, c, y)
        )

    def z_term(k):
        return copy(z_out.at[k], z_in.at[k], z_send.at[k], z_recv.at[k], dev(chunk(k), x, c, y))

    normalize(0)
    pl.semaphore_wait(barrier, 16)
    for k in range(2):
        if k:
            normalize(k)
        direct(k, 0).start()
        direct(k, 1).start()
        if k == 0:
            for r in range(1, 8):
                w_first(r).start()
            cot_swap().start()

    acc[...] = jnp.zeros_like(acc)
    mine = cot[pl.ds(pl.multiple_of(xl * group, group), group), :]
    cot_t[pl.ds(0, side), :] = mine.T
    cot_swap().wait_recv()
    cot_t[pl.ds(side, side), :] = cot_in[...].T

    for r in range(1, 8):
        w_first_in(r).wait_recv()
    w_ring(0, zp, 7).start()
    w_ring(0, zm, 1).start()

    def products(k, other, first):
        zc, slot = chunk(k), lax.rem(k, 2)

        @pl.loop(0, 2)
        def _(h):
            j = h * 2 + other
            n = normed[zc, :, j].reshape(group, side)
            d = jnp.dot(cot_t[...], n, preferred_element_type=jnp.float32)
            part[slot, first + h] = d.reshape(2, side, side)
            for u in range(2):
                w = masked[zc, j, lax.rem(xl + u, 2)]
                acc[u] += jnp.dot(n, w, preferred_element_type=jnp.float32)

    @pl.loop(0, NZ + 3)
    def _(i):
        @pl.when(i < NZ)
        def _():
            for way in range(2):
                direct_in(i, way).wait_recv()
                forward(i, way).start()
            for way in range(2):
                direct(i, way).wait_send()

            @pl.when(i < NZ - 2)
            def _():
                normalize(i + 2)
                direct(i + 2, 0).start()
                direct(i + 2, 1).start()

        @pl.when(i < 4)
        def _():
            w_ring_in(7 - i).wait_recv()
            w_share(7 - i).start()

            @pl.when(i < 3)
            def _():
                w_ring(7 - i, zp, 6 - i).start()
                w_ring_in(i + 1).wait_recv()
                w_share(i + 1).start()

            @pl.when(i < 2)
            def _():
                w_ring(i + 1, zm, i + 2).start()

        @pl.when((i >= 1) & (i <= NZ))
        def _():
            k = i - 1
            forward_in(k, 0).wait_recv()
            forward_in(k, 1).wait_recv()

            @pl.when(k < NZ - 1)
            def _():
                w_share_in(k + 1).wait_recv()

            @pl.when(k >= 2)
            def _():
                core_swap(k - 2).wait_send()

            products(k, 1 - c, 0)
            core_swap(k).start()
            products(k, c, 2)

            @pl.when(k == NZ - 1)
            def _():
                p_out[...] = acc[1].astype(jnp.bfloat16)
                proj_swap().start()

        @pl.when((i >= 2) & (i <= NZ + 1))
        def _():
            k = i - 2
            slot = lax.rem(k, 2)
            core_swap(k).wait_recv()
            for d in range(1, NX):
                xd = lax.rem(x + d, NX)
                h, u = lax.div(xd, 2), lax.rem(xd + xl, 2)
                x_out[k, d - 1] = (part[slot, 2 + h, u] + core_in[k, h, u]).astype(jnp.bfloat16)
                x_term(k, d).start()
            keep[slot] = part[slot, 2 + xh, 0] + core_in[k, xh, 0]

        @pl.when(i >= 3)
        def _():
            k = i - 3
            slot = lax.rem(k, 2)
            for d in range(1, NX):
                x_term(k, d).wait_recv()
            terms = [x_in[k, d].astype(jnp.float32) for d in range(NX - 1)]
            total = keep[slot] + (terms[0] + terms[1] + terms[2])

            @pl.when(k < NZ - 1)
            def _():
                z_out[k] = total
                z_term(k).start()

            @pl.when(k == NZ - 1)
            def _():
                keep[slot] = total

    for k in range(NZ - 1):
        z_term(k).wait_recv()
    total = keep[(NZ - 1) % 2]
    for k in range(NZ - 1):
        total = total + z_in[k]
    total = total.T
    for a in range(side // BLOCK):
        for b in range(side // BLOCK):
            m = mask[a, b].astype(jnp.float32)
            grad[pl.ds(a * BLOCK, BLOCK), pl.ds(b * BLOCK, BLOCK)] = (
                total[a * BLOCK : (a + 1) * BLOCK, b * BLOCK : (b + 1) * BLOCK] * m
            )

    proj[pl.ds(pl.multiple_of(xl * group, group), group), :] = acc[0].astype(jnp.bfloat16)
    proj_swap().wait_recv()
    proj[pl.ds(pl.multiple_of((1 - xl) * group, group), group), :] = p_in[...]

    @pl.loop(0, NZ)
    def _(k):
        forward(k, 0).wait_send()
        forward(k, 1).wait_send()
        for d in range(1, NX):
            x_term(k, d).wait_send()

    @pl.loop(0, NZ - 1)
    def _(k):
        w_first(k + 1).wait_send()
        w_ring_in(k + 1).wait_send()
        w_share(k + 1).wait_send()
        z_term(k).wait_send()

    core_swap(NZ - 2).wait_send()
    core_swap(NZ - 1).wait_send()
    cot_swap().wait_send()
    proj_swap().wait_send()


def per_device(tokens, gain, kv_weight, block_mask, cotangent):
    rows, width = tokens.shape
    side = kv_weight.shape[0]
    group = NY * rows
    bf16, f32 = jnp.bfloat16, jnp.float32
    dma = pltpu.SemaphoreType.DMA
    vmem = pl.BlockSpec(memory_space=pltpu.VMEM)
    pairs = [(NZ, 4), (8,), (NZ,), (NZ,), (NZ,), (NZ, 3), (NZ,), (2,)]
    return pl.pallas_call(
        kernel,
        out_shape=(
            jax.ShapeDtypeStruct(cotangent.shape, bf16),
            jax.ShapeDtypeStruct(kv_weight.shape, f32),
        ),
        in_specs=[vmem, vmem, vmem, pl.BlockSpec(memory_space=pltpu.SMEM), vmem],
        out_specs=(vmem, vmem),
        scratch_shapes=[
            pltpu.VMEM((NZ, NY, 4, rows, side), bf16),
            pltpu.VMEM((rows, side), f32),
            pltpu.VMEM((NZ, 4, 2, side, side), bf16),
            pltpu.VMEM((group, side), bf16),
            pltpu.VMEM((2 * side, group), bf16),
            pltpu.VMEM((2, 4, 2, side, side), f32),
            pltpu.VMEM((NZ, 2, 2, side, side), f32),
            pltpu.VMEM((2, side, side), f32),
            pltpu.VMEM((NZ, NX - 1, side, side), bf16),
            pltpu.VMEM((NZ, NX - 1, side, side), bf16),
            pltpu.VMEM((NZ - 1, side, side), f32),
            pltpu.VMEM((NZ - 1, side, side), f32),
            pltpu.VMEM((2, group, side), f32),
            pltpu.VMEM((group, side), bf16),
            pltpu.VMEM((group, side), bf16),
        ]
        + [dma(shape) for shape in pairs for _ in range(2)],
        compiler_params=pltpu.CompilerParams(
            collective_id=0, has_side_effects=True, vmem_limit_bytes=60 * 1024 * 1024
        ),
        cost_estimate=pl.CostEstimate(
            flops=8 * group * width * side, bytes_accessed=2 * rows * width, transcendentals=rows
        ),
    )(tokens, gain.reshape(1, width), kv_weight, block_mask, cotangent)


def solution(mesh):
    return jax.shard_map(
        per_device,
        mesh=mesh,
        in_specs=(
            P(("fsdp", "tensor"), None),
            P(),
            P("fsdp", "tensor"),
            P("fsdp", "tensor"),
            P("fsdp", "tensor"),
        ),
        out_specs=(P("fsdp", "tensor"), P("fsdp", "tensor")),
        check_vma=False,
    )
```

time: 521 us -> 162 us (0.31)
  waiting for transfers between devices: 421 us -> 0 us
  Pallas kernels: 0 us -> 156 us
  blocking collectives: 42.3 us -> 0 us
  matrix products: 27.5 us -> 0 us
  between operations: 13.8 us -> 0.64 us
  other arithmetic: 9.57 us -> 0 us
    all_gather x2 -> x0, waiting for transfers between devices: 287 us -> none  [the longest x1 255 us: per_device(): lax.all_gather(normalize(tokens, gain), 'tensor', axis=0, tiled=True)]
    pallas_call x0 -> x1, Pallas kernels: none -> 156 us  [per_device(): pl.pallas_call(kernel, out_shape=(jax.ShapeDtypeStruct(cotangent.shape, b...]
    reduce_scatter x1 -> x0, waiting for transfers between devices: 134 us -> none  [per_device(): lax.psum_scatter(lax.dot_general(columns, cotangent, (((0,), (0,)), ((),...]
    all_gather x1 -> x0, blocking collectives: 42.3 us -> none  [per_device(): lax.all_gather(block_mask, 'fsdp', axis=0, tiled=True)]
    dot_general x2 -> x0, matrix products: 27.5 us -> none  [the longest x1 13.9 us: per_device(): lax.dot_general(columns, cotangent, (((0,), (0,)), ((), ())), preferred_e...]
    convert_element_type x4 -> x0, other arithmetic: 5.27 us -> none  [the longest x1 4.48 us: normalize(): (values * lax.rsqrt(square + 1e-05) * gain.astype(jnp.float32)).astype(jn...]
  transfers between devices with their start and end apart: 3 -> 0, of which waited for: 3 -> 0; matrix products, arithmetic and copies ran while one was open for 6% -> 0% of each run, Pallas kernels for 0% -> 0%
where the time goes in v1:
time: 162 us; the launch traced here: 161 us
  Pallas kernels  156 us (96%)
  local copies, waits for them, and re-layouts  5.08 us (3%)
    pallas_call x1, Pallas kernels, per_device(): pl.pallas_call(kernel, out_shape=(jax.ShapeDtypeStruct(cotangent.shape, b...  156 us
    unnamed x2, local copies, waits for them, and re-layouts  3.73 us

profile of v1, /device:TPU:1, one launch (start us, length us, event | category | flops | bytes accessed | tf_op | source)
XLA Modules:
  0.0 161.4 jit_solution(2238687276222695742)
XLA Ops:
  0.6 1.4 reshape.7.gain
  2.0 155.7 %shard_map.68 = (bf16[1536,256]{1,0:T(8,128)(2,1)}, f32[256,256]{1,0:T(8,128)}) custom-call(bf16[192,8192]{1,0:T(8,128)(2,1)} %tokens.1, bf16[1,8192]{1,0:T(2,128)(2,1)} %reshape.7.gain, bf16[256,256]{1,0:T(8,128)(2,1)} %weight.1, s32[2,2]{1,0:T(2,128)} %mask.1, bf16[1536,256]{1,0:T(8,128)(2,1)} %cot.1), custom_call_target="tpu_custom_call" | custom-call | flops 12884901888 | bytes 3145728 | tf_op jit(solution)/shard_map/pallas_call | solution.py:316
  157.7 2.1 %copy.9 = bf16[1536,256]{1,0:T(8,128)(2,1)} copy(bf16[1536,256]{1,0:T(8,128)(2,1)} %get-tuple-element.4) | data formatting | bytes 1572864
  159.7 1.7 %copy.10 = f32[256,256]{1,0:T(8,128)} copy(f32[256,256]{1,0:T(8,128)} %get-tuple-element.5) | data formatting | bytes 524288

commit v2 on v1

v2 whole, which is shorter than its diff:
```python
import jax
import jax.numpy as jnp
from jax import lax
from jax.experimental import pallas as pl
from jax.experimental.pallas import tpu as pltpu
from jax.sharding import PartitionSpec as P

MESH = pl.DeviceIdType.MESH
NZ, NX, NC, NY = 8, 4, 2, 4
BLOCK = 128
AHEAD = 3


def kernel(
    tokens, gain, weight, mask, cot, proj, grad,
    normed, scale, masked, cot_in, cot_t, part, core_in, keep, x_out, x_in,
    z_out, z_in, acc, p_out, p_in,
    y_send, y_recv, w_send, w_recv, wz_send, wz_recv, wd_send, wd_recv,
    c_send, c_recv, x_send, x_recv, z_send, z_recv, o_send, o_recv,
):
    rows = tokens.shape[0]
    group = NY * rows
    side = weight.shape[0]
    wide = 4 * side
    steps = 2 * NZ
    f, t = lax.axis_index("fsdp"), lax.axis_index("tensor")
    z, xh, c = lax.div(f, 4), lax.rem(lax.div(f, 2), 2), lax.rem(f, 2)
    xl, y = lax.div(t, NY), lax.rem(t, NY)
    x = xh * 2 + xl
    q = x * 2 + c
    yp, ym, y2 = lax.rem(y + 1, NY), lax.rem(y + 3, NY), lax.rem(y + 2, NY)
    zp, zm = lax.rem(z + 1, NZ), lax.rem(z + NZ - 1, NZ)

    def dev(zz, xx, cc, yy):
        return ((zz * 2 + lax.div(xx, 2)) * 2 + cc, lax.rem(xx, 2) * NY + yy)

    def chunk(m):
        return lax.rem(z + 1 + m, NZ)

    def half(k):
        return chunk(lax.div(k, 2)), lax.rem(xh + 1 + k, 2)

    def copy(src, dst, send, recv, to):
        return pltpu.make_async_remote_copy(
            src_ref=src, dst_ref=dst, send_sem=send, recv_sem=recv, device_id=to, device_id_type=MESH
        )

    sibling = dev(z, x, 1 - c, y)
    beside = dev(z, xh * 2 + 1 - xl, c, y)
    up, down = dev(z, x, c, yp), dev(z, x, c, ym)

    barrier = pltpu.get_barrier_semaphore()

    def greet(to):
        pl.semaphore_signal(barrier, inc=1, device_id=to, device_id_type=MESH)

    greet(up)
    greet(down)
    for r in range(1, 8):
        p = lax.rem(q + r, 8)
        greet(dev(z, lax.div(p, 2), lax.rem(p, 2), y))
        greet(dev(lax.rem(z + r, NZ), x, c, y))

    own_j = xh * 2 + c
    for a in range(side // BLOCK):
        for b in range(side // BLOCK):
            at = (pl.ds(a * BLOCK, BLOCK), pl.ds(b * BLOCK, BLOCK))
            m = mask[a, b].astype(jnp.float32)
            masked[z, own_j, xl, at[0], at[1]] = (weight[at].astype(jnp.float32) * m).astype(jnp.bfloat16)

    @pl.loop(0, rows // 16)
    def _(r):
        at = pl.ds(pl.multiple_of(r * 16, 16), 16)
        v = tokens[at, :].astype(jnp.float32)
        square = jnp.mean(v * v, axis=-1, keepdims=True)
        scale[at, :] = jnp.broadcast_to(lax.rsqrt(square + 1e-05), (16, side))

    def normalize(k):
        zc, h = half(k)

        @pl.loop(0, 2)
        def _(e):
            at = pl.ds(pl.multiple_of(zc * wide + (2 * h + e) * side, side), side)
            v = tokens[:, at].astype(jnp.float32)
            g = gain[at].astype(jnp.float32).reshape(1, side)
            normed[zc, y, 2 * h + e] = (v * scale[...] * g).astype(jnp.bfloat16)

    def direct(k, way):
        zc, h = half(k)
        slot = normed.at[zc, y, pl.ds(2 * h, 2)]
        return copy(slot, slot, y_send.at[k, way], y_recv.at[k, way], down if way else up)

    def direct_in(k, way):
        zc, h = half(k)
        slot = normed.at[zc, yp if way else ym, pl.ds(2 * h, 2)]
        return copy(slot, slot, y_send.at[k, way], y_recv.at[k, way], up)

    def forward(k, way):
        zc, h = half(k)
        slot = normed.at[zc, yp if way else ym, 2 * h + way]
        return copy(slot, slot, y_send.at[k, 2 + way], y_recv.at[k, 2 + way], down if way else up)

    def forward_in(k, way):
        zc, h = half(k)
        slot = normed.at[zc, y2, 2 * h + way]
        return copy(slot, slot, y_send.at[k, 2 + way], y_recv.at[k, 2 + way], up)

    def w_first(r):
        p = lax.rem(q + r, 8)
        slot = masked.at[z, own_j, xl]
        return copy(slot, slot, w_send.at[r], w_recv.at[r], dev(z, lax.div(p, 2), lax.rem(p, 2), y))

    def w_first_in(r):
        p = lax.rem(q + 8 - r, 8)
        px, pc = lax.div(p, 2), lax.rem(p, 2)
        slot = masked.at[z, lax.div(px, 2) * 2 + pc, lax.rem(px, 2)]
        return copy(slot, slot, w_send.at[r], w_recv.at[r], sibling)

    def w_ring(offset, to, at_receiver):
        slot = masked.at[lax.rem(z + offset, NZ), pl.ds(2 * c, 2)]
        return copy(slot, slot, wz_send.at[at_receiver], wz_recv.at[at_receiver], dev(to, x, c, y))

    def w_ring_in(offset):
        return w_ring(offset, zp, offset)

    def w_share(offset):
        slot = masked.at[lax.rem(z + offset, NZ), pl.ds(2 * c, 2)]
        return copy(slot, slot, wd_send.at[offset], wd_recv.at[offset], sibling)

    def w_share_in(offset):
        slot = masked.at[lax.rem(z + offset, NZ), pl.ds(2 * (1 - c), 2)]
        return copy(slot, slot, wd_send.at[offset], wd_recv.at[offset], sibling)

    def cot_swap():
        src = cot.at[pl.ds(pl.multiple_of((1 - xl) * group, group), group)]
        return copy(src, cot_in, o_send.at[NY], o_recv.at[NY], beside)

    def proj_swap(away):
        at = lax.rem(y + away, NY)
        return copy(p_out.at[at], p_in.at[at], o_send.at[away], o_recv.at[away], beside)

    def core_swap(k):
        return copy(part.at[lax.rem(k, 2), 0], core_in.at[k], c_send.at[k], c_recv.at[k], sibling)

    def x_term(m, d):
        to = dev(z, (xh if d == 2 else 1 - xh) * 2 + (1 - xl if d else xl), c, y)
        return copy(x_out.at[m, d], x_in.at[m, d], x_send.at[m, d], x_recv.at[m, d], to)

    def z_term(m):
        return copy(z_out.at[m], z_in.at[m], z_send.at[m], z_recv.at[m], dev(chunk(m), x, c, y))

    def send(k):
        direct(k, 0).start()
        direct(k, 1).start()

    def relay(k):
        for way in range(2):
            direct_in(k, way).wait_recv()
            forward(k, way).start()

    def products(k):
        zc, h = half(k)
        slot = lax.rem(k, 2)
        forward_in(k, 0).wait_recv()
        forward_in(k, 1).wait_recv()
        for own in range(2):
            n = normed[zc, :, 2 * h + (c if own else 1 - c)].reshape(group, side)
            d = jnp.dot(cot_t[...], n, preferred_element_type=jnp.float32)
            part[slot, own] = d.reshape(2, side, side)
            if not own:
                core_swap(k).start()

    def add_cores(k, far):
        m, slot = lax.div(k, 2), lax.rem(k, 2)
        core_swap(k).wait()
        if far:
            for u in range(2):
                x_out[m, u] = (part[slot, 1, u] + core_in[k, u]).astype(jnp.bfloat16)
                x_term(m, u).start()
        else:
            x_out[m, 2] = (part[slot, 1, 1] + core_in[k, 1]).astype(jnp.bfloat16)
            x_term(m, 2).start()
            keep[lax.rem(m, 2)] = part[slot, 1, 0] + core_in[k, 0]

    def gradient_block(m):
        for d in range(3):
            x_term(m, d).wait_recv()
        terms = [x_in[m, d].astype(jnp.float32) for d in range(3)]
        return keep[lax.rem(m, 2)] + (terms[0] + terms[1] + terms[2])

    def project(m):
        zc = chunk(m)

        @pl.loop(0, 4)
        def _(j):
            n = normed[zc, :, j].reshape(group, side)
            for u in range(2):
                w = masked[zc, j, lax.rem(xl + u, 2)]
                d = jnp.dot(n, w, preferred_element_type=jnp.float32)
                acc[u] += d.reshape(NY, rows, side)

    def project_rows(k, at):
        zc, h = half(k)
        for e in range(2):
            n = normed[zc, at, 2 * h + e]
            for u in range(2):
                w = masked[zc, 2 * h + e, lax.rem(xl + u, 2)]
                acc[u, at] += jnp.dot(n, w, preferred_element_type=jnp.float32)

    normalize(0)
    pl.semaphore_wait(barrier, 16)
    send(0)
    for r in range(1, 8):
        w_first(r).start()
    cot_swap().start()
    for k in range(1, AHEAD):
        normalize(k)
        send(k)

    acc[...] = jnp.zeros_like(acc)
    mine = cot[pl.ds(pl.multiple_of(xl * group, group), group), :]
    cot_t[pl.ds(0, side), :] = mine.T

    @pl.loop(0, NZ)
    def _(m):
        for e in range(2):
            k = 2 * m + e
            relay(k)
            for way in range(2):
                direct(k, way).wait_send()

            @pl.when(k < steps - AHEAD)
            def _():
                normalize(k + AHEAD)
                send(k + AHEAD)

            if e == 0:

                @pl.when(m == 1)
                def _():
                    cot_swap().wait_recv()
                    cot_t[pl.ds(side, side), :] = cot_in[...].T

                @pl.when((m >= 2) & (m <= 5))
                def _():
                    hop = m - 1
                    w_ring_in(8 - hop).wait_recv()
                    w_share(8 - hop).start()

                    @pl.when(hop < 4)
                    def _():
                        w_ring(8 - hop, zp, 7 - hop).start()
                        w_ring_in(hop).wait_recv()
                        w_share(hop).start()

                    @pl.when(hop < 3)
                    def _():
                        w_ring(hop, zm, hop + 1).start()

                @pl.when(m >= 3)
                def _():
                    z_out[m - 3] = gradient_block(m - 3).astype(z_out.dtype)
                    z_term(m - 3).start()

                @pl.when(m >= 2)
                def _():
                    add_cores(k - 3, False)

                @pl.when(m >= 1)
                def _():
                    products(k - 2)

                @pl.when(m == NZ - 1)
                def _():
                    w_share_in(NZ - 2).wait_recv()
                    project(NZ - 3)
                    w_share_in(NZ - 1).wait_recv()
                    for n in range(-2, 2):
                        project_rows(k + n, y)
                    p_out[y] = acc[1, y].astype(jnp.bfloat16)
                    proj_swap(0).start()

            else:

                @pl.when(m == 0)
                def _():
                    for r in range(1, 8):
                        w_first_in(r).wait_recv()
                    w_ring(0, zp, 7).start()
                    w_ring(0, zm, 1).start()

                @pl.when((m >= 2) & (m < NZ - 1))
                def _():
                    w_share_in(m - 1).wait_recv()
                    project(m - 2)

                @pl.when(m == NZ - 1)
                def _():
                    z_out[NZ - 3] = gradient_block(NZ - 3).astype(z_out.dtype)
                    z_term(NZ - 3).start()

                @pl.when(m >= 1)
                def _():
                    add_cores(k - 3, True)

                @pl.when(m == NZ - 1)
                def _():
                    for away in (1, 3):
                        at = lax.rem(y + away, NY)
                        for n in range(-3, 1):
                            project_rows(k + n, at)
                        p_out[at] = acc[1, at].astype(jnp.bfloat16)
                        proj_swap(away).start()

                @pl.when(m >= 1)
                def _():
                    products(k - 2)

    last = steps - 1
    products(last - 1)
    add_cores(last - 2, False)
    products(last)
    add_cores(last - 1, True)
    for k in range(last - 3, last + 1):
        project_rows(k, y2)
    p_out[y2] = acc[1, y2].astype(jnp.bfloat16)
    add_cores(last, False)
    proj_swap(2).start()
    z_out[NZ - 2] = gradient_block(NZ - 2).astype(z_out.dtype)
    z_term(NZ - 2).start()
    proj[pl.ds(pl.multiple_of(xl * group, group), group), :] = acc[0].reshape(group, side).astype(jnp.bfloat16)

    total = gradient_block(NZ - 1)
    for m in range(NZ - 1):
        z_term(m).wait_recv()
        total = total + z_in[m].astype(jnp.float32)
    total = total.T
    for a in range(side // BLOCK):
        for b in range(side // BLOCK):
            m = mask[a, b].astype(jnp.float32)
            grad[pl.ds(a * BLOCK, BLOCK), pl.ds(b * BLOCK, BLOCK)] = (
                total[a * BLOCK : (a + 1) * BLOCK, b * BLOCK : (b + 1) * BLOCK] * m
            )

    for away in (0, 1, 3, 2):
        proj_swap(away).wait_recv()
    proj[pl.ds(pl.multiple_of((1 - xl) * group, group), group), :] = p_in[...].reshape(group, side)

    @pl.loop(0, steps)
    def _(k):
        forward(k, 0).wait_send()
        forward(k, 1).wait_send()

    @pl.loop(0, NZ)
    def _(m):
        for d in range(3):
            x_term(m, d).wait_send()

    @pl.loop(0, NZ - 1)
    def _(m):
        w_first(m + 1).wait_send()
        w_ring_in(m + 1).wait_send()
        w_share(m + 1).wait_send()
        z_term(m).wait_send()

    cot_swap().wait_send()
    for away in range(NY):
        proj_swap(away).wait_send()


def per_device(tokens, gain, kv_weight, block_mask, cotangent):
    rows, width = tokens.shape
    side = kv_weight.shape[0]
    group = NY * rows
    bf16, f32 = jnp.bfloat16, jnp.float32
    dma = pltpu.SemaphoreType.DMA
    vmem = pl.BlockSpec(memory_space=pltpu.VMEM)
    pairs = [(2 * NZ, 4), (8,), (NZ,), (NZ,), (2 * NZ,), (NZ, 3), (NZ,), (NY + 1,)]
    return pl.pallas_call(
        kernel,
        out_shape=(
            jax.ShapeDtypeStruct(cotangent.shape, bf16),
            jax.ShapeDtypeStruct(kv_weight.shape, f32),
        ),
        in_specs=[vmem, vmem, vmem, pl.BlockSpec(memory_space=pltpu.SMEM), vmem],
        out_specs=(vmem, vmem),
        scratch_shapes=[
            pltpu.VMEM((NZ, NY, 4, rows, side), bf16),
            pltpu.VMEM((rows, side), f32),
            pltpu.VMEM((NZ, 4, 2, side, side), bf16),
            pltpu.VMEM((group, side), bf16),
            pltpu.VMEM((2 * side, group), bf16),
            pltpu.VMEM((2, 2, 2, side, side), f32),
            pltpu.VMEM((2 * NZ, 2, side, side), f32),
            pltpu.VMEM((2, side, side), f32),
            pltpu.VMEM((NZ, 3, side, side), bf16),
            pltpu.VMEM((NZ, 3, side, side), bf16),
            pltpu.VMEM((NZ - 1, side, side), bf16),
            pltpu.VMEM((NZ - 1, side, side), bf16),
            pltpu.VMEM((2, NY, rows, side), f32),
            pltpu.VMEM((NY, rows, side), bf16),
            pltpu.VMEM((NY, rows, side), bf16),
        ]
        + [dma(shape) for shape in pairs for _ in range(2)],
        compiler_params=pltpu.CompilerParams(
            collective_id=0, has_side_effects=True, vmem_limit_bytes=60 * 1024 * 1024
        ),
        cost_estimate=pl.CostEstimate(
            flops=8 * group * width * side, bytes_accessed=2 * rows * width, transcendentals=rows
        ),
    )(tokens, gain, kv_weight, block_mask, cotangent)


def solution(mesh):
    return jax.shard_map(
        per_device,
        mesh=mesh,
        in_specs=(
            P(("fsdp", "tensor"), None),
            P(),
            P("fsdp", "tensor"),
            P("fsdp", "tensor"),
            P("fsdp", "tensor"),
        ),
        out_specs=(P("fsdp", "tensor"), P("fsdp", "tensor")),
        check_vma=False,
    )
```

time: 162 us -> 136 us (0.84)
  Pallas kernels: 156 us -> 131 us
    pallas_call x1, Pallas kernels: 156 us -> 131 us  [per_device(): pl.pallas_call(kernel, out_shape=(jax.ShapeDtypeStruct(cotangent.shape, b...]
where the time goes in v2:
time: 136 us
  Pallas kernels  131 us (96%)
  local copies, waits for them, and re-layouts  3.73 us (3%)
    pallas_call x1, Pallas kernels, per_device(): pl.pallas_call(kernel, out_shape=(jax.ShapeDtypeStruct(cotangent.shape, b...  131 us
    unnamed x2, local copies, waits for them, and re-layouts  3.73 us

profile of v2, /device:TPU:1, one launch (start us, length us, event | category | flops | bytes accessed | tf_op | source)
XLA Modules:
  0.0 135.9 jit_solution(15949167745770243909)
XLA Ops:
  0.6 131.5 %shard_map.68 = (bf16[1536,256]{1,0:T(8,128)(2,1)}, f32[256,256]{1,0:T(8,128)}) custom-call(bf16[192,8192]{1,0:T(8,128)(2,1)} %tokens.1, bf16[8192]{0:T(1024)(128)(2,1)} %gain.1, bf16[256,256]{1,0:T(8,128)(2,1)} %weight.1, s32[2,2]{1,0:T(2,128)} %mask.1, bf16[1536,256]{1,0:T(8,128)(2,1)} %cot.1), custom_call_target="tpu_custom_call" | custom-call | flops 12884901888 | bytes 3145728 | tf_op jit(solution)/shard_map/pallas_call | solution.py:379
  132.1 2.1 %copy.9 = bf16[1536,256]{1,0:T(8,128)(2,1)} copy(bf16[1536,256]{1,0:T(8,128)(2,1)} %get-tuple-element.4) | data formatting | bytes 1572864
  134.2 1.7 %copy.10 = f32[256,256]{1,0:T(8,128)} copy(f32[256,256]{1,0:T(8,128)} %get-tuple-element.5) | data formatting | bytes 524288

commit v3 on v2

--- a/solution.py
+++ b/solution.py
@@ -12,11 +12,11 @@
 
 
 def kernel(
-    tokens, gain, weight, mask, cot, proj, grad,
-    normed, scale, masked, cot_in, cot_t, part, core_in, keep, x_out, x_in,
+    tokens_in, gain, weight, mask, cot, proj, grad,
+    tokens, normed, scale, masked, cot_in, cot_t, part, core_in, keep, x_out, x_in,
     z_out, z_in, acc, p_out, p_in,
     y_send, y_recv, w_send, w_recv, wz_send, wz_recv, wd_send, wd_recv,
-    c_send, c_recv, x_send, x_recv, z_send, z_recv, o_send, o_recv,
+    c_send, c_recv, x_send, x_recv, z_send, z_recv, o_send, o_recv, load_sem,
 ):
     rows = tokens.shape[0]
     group = NY * rows
@@ -49,6 +49,15 @@
     beside = dev(z, xh * 2 + 1 - xl, c, y)
     up, down = dev(z, x, c, yp), dev(z, x, c, ym)
 
+    quarter = rows // 4
+
+    def load(n):
+        at = pl.ds(n * quarter, quarter)
+        return pltpu.make_async_copy(tokens_in.at[at], tokens.at[at], load_sem.at[n])
+
+    for n in range(4):
+        load(n).start()
+
     barrier = pltpu.get_barrier_semaphore()
 
     def greet(to):
@@ -68,12 +77,15 @@
             m = mask[a, b].astype(jnp.float32)
             masked[z, own_j, xl, at[0], at[1]] = (weight[at].astype(jnp.float32) * m).astype(jnp.bfloat16)
 
-    @pl.loop(0, rows // 16)
-    def _(r):
-        at = pl.ds(pl.multiple_of(r * 16, 16), 16)
-        v = tokens[at, :].astype(jnp.float32)
-        square = jnp.mean(v * v, axis=-1, keepdims=True)
-        scale[at, :] = jnp.broadcast_to(lax.rsqrt(square + 1e-05), (16, side))
+    for n in range(4):
+        load(n).wait()
+
+        @pl.loop(n * quarter // 16, (n + 1) * quarter // 16)
+        def _(r):
+            at = pl.ds(pl.multiple_of(r * 16, 16), 16)
+            v = tokens[at, :].astype(jnp.float32)
+            square = jnp.mean(v * v, axis=-1, keepdims=True)
+            scale[at, :] = jnp.broadcast_to(lax.rsqrt(square + 1e-05), (16, side))
 
     def normalize(k):
         zc, h = half(k)
@@ -272,13 +284,9 @@
 
                 @pl.when(m == NZ - 1)
                 def _():
-                    w_share_in(NZ - 2).wait_recv()
-                    project(NZ - 3)
-                    w_share_in(NZ - 1).wait_recv()
-                    for n in range(-2, 2):
-                        project_rows(k + n, y)
-                    p_out[y] = acc[1, y].astype(jnp.bfloat16)
-                    proj_swap(0).start()
+                    for away in (1, 3):
+                        for n in range(-4, 0):
+                            project_rows(k + n, lax.rem(y + away, NY))
 
             else:
 
@@ -294,6 +302,15 @@
                     w_share_in(m - 1).wait_recv()
                     project(m - 2)
 
+                @pl.when(m == NZ - 2)
+                def _():
+                    w_share_in(NZ - 2).wait_recv()
+                    w_share_in(NZ - 1).wait_recv()
+                    for n in range(-3, 3):
+                        project_rows(k + n, y)
+                    p_out[y] = acc[1, y].astype(jnp.bfloat16)
+                    proj_swap(0).start()
+
                 @pl.when(m == NZ - 1)
                 def _():
                     z_out[NZ - 3] = gradient_block(NZ - 3).astype(z_out.dtype)
@@ -307,7 +324,7 @@
                 def _():
                     for away in (1, 3):
                         at = lax.rem(y + away, NY)
-                        for n in range(-3, 1):
+                        for n in range(-1, 1):
                             project_rows(k + n, at)
                         p_out[at] = acc[1, at].astype(jnp.bfloat16)
                         proj_swap(away).start()
@@ -319,12 +336,13 @@
     last = steps - 1
     products(last - 1)
     add_cores(last - 2, False)
+    for k in range(last - 5, last):
+        project_rows(k, y2)
+    add_cores(last - 1, True)
     products(last)
-    add_cores(last - 1, True)
-    for k in range(last - 3, last + 1):
-        project_rows(k, y2)
+    add_cores(last, False)
+    project_rows(last, y2)
     p_out[y2] = acc[1, y2].astype(jnp.bfloat16)
-    add_cores(last, False)
     proj_swap(2).start()
     z_out[NZ - 2] = gradient_block(NZ - 2).astype(z_out.dtype)
     z_term(NZ - 2).start()
@@ -368,6 +386,11 @@
         proj_swap(away).wait_send()
 
 
+def hand_over(proj_in, grad_in, proj, grad):
+    proj[...] = proj_in[...]
+    grad[...] = grad_in[...]
+
+
 def per_device(tokens, gain, kv_weight, block_mask, cotangent):
     rows, width = tokens.shape
     side = kv_weight.shape[0]
@@ -376,15 +399,16 @@
     dma = pltpu.SemaphoreType.DMA
     vmem = pl.BlockSpec(memory_space=pltpu.VMEM)
     pairs = [(2 * NZ, 4), (8,), (NZ,), (NZ,), (2 * NZ,), (NZ, 3), (NZ,), (NY + 1,)]
-    return pl.pallas_call(
+    results = pl.pallas_call(
         kernel,
         out_shape=(
             jax.ShapeDtypeStruct(cotangent.shape, bf16),
             jax.ShapeDtypeStruct(kv_weight.shape, f32),
         ),
-        in_specs=[vmem, vmem, vmem, pl.BlockSpec(memory_space=pltpu.SMEM), vmem],
+        in_specs=[pl.BlockSpec(memory_space=pl.ANY), vmem, vmem, pl.BlockSpec(memory_space=pltpu.SMEM), vmem],
         out_specs=(vmem, vmem),
         scratch_shapes=[
+            pltpu.VMEM((rows, width), bf16),
             pltpu.VMEM((NZ, NY, 4, rows, side), bf16),
             pltpu.VMEM((rows, side), f32),
             pltpu.VMEM((NZ, 4, 2, side, side), bf16),
@@ -401,7 +425,8 @@
             pltpu.VMEM((NY, rows, side), bf16),
             pltpu.VMEM((NY, rows, side), bf16),
         ]
-        + [dma(shape) for shape in pairs for _ in range(2)],
+        + [dma(shape) for shape in pairs for _ in range(2)]
+        + [dma((4,))],
         compiler_params=pltpu.CompilerParams(
             collective_id=0, has_side_effects=True, vmem_limit_bytes=60 * 1024 * 1024
         ),
@@ -409,6 +434,12 @@
             flops=8 * group * width * side, bytes_accessed=2 * rows * width, transcendentals=rows
         ),
     )(tokens, gain, kv_weight, block_mask, cotangent)
+    return pl.pallas_call(
+        hand_over,
+        out_shape=tuple(jax.ShapeDtypeStruct(r.shape, r.dtype) for r in results),
+        in_specs=[vmem] * 2,
+        out_specs=(vmem,) * 2,
+    )(*results)
 
 
 def solution(mesh):

time: 136 us -> 134 us (0.985)
  local copies, waits for them, and re-layouts: 3.73 us -> 0 us
  Pallas kernels: 131 us -> 133 us
    unnamed x2 -> x0, local copies, waits for them, and re-layouts: 3.73 us -> none
    pallas_call x0 -> x1, Pallas kernels: none -> 2.2 us  [per_device(): pl.pallas_call(hand_over, out_shape=tuple((jax.ShapeDtypeStruct(r.shape,...]
where the time goes in v3:
time: 134 us; the launch traced here: 133 us
  Pallas kernels  133 us (99%)
    pallas_call x1, Pallas kernels, per_device(): pl.pallas_call(kernel, out_shape=(jax.ShapeDtypeStruct(cotangent.shape, b...  131 us

profile of v3, /device:TPU:1, one launch (start us, length us, event | category | flops | bytes accessed | tf_op | source)
XLA Modules:
  0.0 133.5 jit_solution(11726885333410478970)
XLA Ops:
  0.6 130.7 %shard_map.68 = (bf16[1536,256]{1,0:T(8,128)(2,1)}, f32[256,256]{1,0:T(8,128)}) custom-call(bf16[192,8192]{1,0:T(8,128)(2,1)} %tokens_in.1, bf16[8192]{0:T(1024)(128)(2,1)} %gain.1, bf16[256,256]{1,0:T(8,128)(2,1)} %weight.1, s32[2,2]{1,0:T(2,128)} %mask.1, bf16[1536,256]{1,0:T(8,128)(2,1)} %cot.1), custom_call_target="tpu_custom_call" | custom-call | flops 12884901888 | bytes 3145728 | tf_op jit(solution)/shard_map/pallas_call | solution.py:402
  131.3 2.2 %shard_map.69 = (bf16[1536,256]{1,0:T(8,128)(2,1)}, f32[256,256]{1,0:T(8,128)}) custom-call(bf16[1536,256]{1,0:T(8,128)(2,1)} %get-tuple-element.4.proj_in, f32[256,256]{1,0:T(8,128)} %get-tuple-element.5.grad_in), custom_call_target="tpu_custom_call" | custom-call | tf_op jit(solution)/shard_map/pallas_call | solution.py:437

commit v4 on v3

--- a/solution.py
+++ b/solution.py
@@ -297,6 +297,15 @@
                     w_ring(0, zp, 7).start()
                     w_ring(0, zm, 1).start()
 
+                @pl.when(m == NZ - 1)
+                def _():
+                    for away in (1, 3):
+                        at = lax.rem(y + away, NY)
+                        for n in range(-1, 1):
+                            project_rows(k + n, at)
+                        p_out[at] = acc[1, at].astype(jnp.bfloat16)
+                        proj_swap(away).start()
+
                 @pl.when((m >= 2) & (m < NZ - 1))
                 def _():
                     w_share_in(m - 1).wait_recv()
@@ -319,15 +328,6 @@
                 @pl.when(m >= 1)
                 def _():
                     add_cores(k - 3, True)
-
-                @pl.when(m == NZ - 1)
-                def _():
-                    for away in (1, 3):
-                        at = lax.rem(y + away, NY)
-                        for n in range(-1, 1):
-                            project_rows(k + n, at)
-                        p_out[at] = acc[1, at].astype(jnp.bfloat16)
-                        proj_swap(away).start()
 
                 @pl.when(m >= 1)
                 def _():

time: 134 us -> 133 us (level)
  no operation moved by 1% of the time
where the time goes in v4:
time: 133 us
  Pallas kernels  133 us (100%)
    pallas_call x1, Pallas kernels, per_device(): pl.pallas_call(kernel, out_shape=(jax.ShapeDtypeStruct(cotangent.shape, b...  130 us

profile of v4, /device:TPU:1, one launch (start us, length us, event | category | flops | bytes accessed | tf_op | source)
XLA Modules:
  0.0 133.3 jit_solution(13949186292723409994)
XLA Ops:
  0.6 130.4 %shard_map.68 = (bf16[1536,256]{1,0:T(8,128)(2,1)}, f32[256,256]{1,0:T(8,128)}) custom-call(bf16[192,8192]{1,0:T(8,128)(2,1)} %tokens_in.1, bf16[8192]{0:T(1024)(128)(2,1)} %gain.1, bf16[256,256]{1,0:T(8,128)(2,1)} %weight.1, s32[2,2]{1,0:T(2,128)} %mask.1, bf16[1536,256]{1,0:T(8,128)(2,1)} %cot.1), custom_call_target="tpu_custom_call" | custom-call | flops 12884901888 | bytes 3145728 | tf_op jit(solution)/shard_map/pallas_call | solution.py:402
  131.1 2.2 %shard_map.69 = (bf16[1536,256]{1,0:T(8,128)(2,1)}, f32[256,256]{1,0:T(8,128)}) custom-call(bf16[1536,256]{1,0:T(8,128)(2,1)} %get-tuple-element.4.proj_in, f32[256,256]{1,0:T(8,128)} %get-tuple-element.5.grad_in), custom_call_target="tpu_custom_call" | custom-call | tf_op jit(solution)/shard_map/pallas_call | solution.py:437
